TPU v7x, 256 devices: a whole 4x4x8 slice. The times are simulated.
256 devices in a mesh: rows: 32 (over z_lo, y, x), cols: 8 (over z_hi, core).
Axes of the slice: x: 4, y: 4, z: 8 (z_hi: 4, z_lo: 2; z = z_hi * 2 + z_lo), core: 2. Of those that a mesh axis runs over, the one named last changes fastest.
Arguments:
- canvas: bfloat16 [256, 1024, 256], P('rows', 'cols'), may hold values from -16 to 16
- conv_weight: bfloat16 [3, 3, 256, 512], replicated, may hold values from -0.125 to 0.125
- conv_bias: bfloat16 [512], replicated, may hold values from -3 to 3
- target_gram: float32 [512, 512], P(('rows', 'cols')), may hold values from -6 to 6
Outputs:
- gram: float32 [512, 512], P(('rows', 'cols'))
- grad_canvas: bfloat16 [256, 1024, 256], P('rows', 'cols')
All inputs are finite; a program needn't handle non-finite values.
Results may differ from a plain program's by a relative error of at most 0.009.
Values may be sent and summed in bfloat16 or wider, within the bound.
A program may use at most 64 MiB of HBM per device.

v0:
```python
import math
import jax
import jax.numpy as jnp
from jax import lax
from jax.sharding import PartitionSpec as P

gelu_scale = math.sqrt(2.0 / math.pi)


def padded_2(block, sides, width):
    for axis, dim in sides:
        count = lax.axis_size(axis)
        forward = [(i, i + 1) for i in range(count - 1)]
        backward = [(target, source) for source, target in forward]
        low = lax.ppermute(
            lax.slice_in_dim(block, block.shape[dim] - width, None, axis=dim), axis, forward
        )
        high = lax.ppermute(lax.slice_in_dim(block, 0, width, axis=dim), axis, backward)
        block = jnp.concatenate([low, block, high], axis=dim)
    return block


def gelu_grad(value):
    tangent = jnp.tanh(gelu_scale * (value + 0.044715 * value * value * value))
    return 0.5 * (1.0 + tangent) + 0.5 * value * (1.0 - tangent * tangent) * gelu_scale * (
        1.0 + 3.0 * 0.044715 * value * value
    )


def patches(padded, tile_rows, tile_cols):
    pieces = [
        padded[row_off : row_off + tile_rows, col_off : col_off + tile_cols, :]
        for row_off in range(3)
        for col_off in range(3)
    ]
    return jnp.concatenate(pieces, axis=2).reshape(tile_rows * tile_cols, -1)


def on_device(canvas, conv_weight, conv_bias, target_gram):
    tile_rows, tile_cols, in_width = canvas.shape
    out_width = conv_weight.shape[3]
    pixel_total = tile_rows * tile_cols * lax.axis_size("rows") * lax.axis_size("cols")
    padded = padded_2(canvas, (("rows", 0), ("cols", 1)), 1)
    kernel = conv_weight.reshape(9 * in_width, out_width)
    preact = jnp.dot(
        patches(padded, tile_rows, tile_cols), kernel, preferred_element_type=jnp.float32
    ) + conv_bias.astype(jnp.float32)
    features = jax.nn.gelu(preact, approximate=True).astype(jnp.bfloat16)
    gram_own = (
        lax.psum_scatter(
            lax.dot_general(
                features, features, (((0,), (0,)), ((), ())), preferred_element_type=jnp.float32
            ),
            ("rows", "cols"),
            scatter_dimension=0,
            tiled=True,
        )
        / pixel_total
    )
    error_own = gram_own - target_gram
    error_full = lax.all_gather(error_own, ("rows", "cols"), axis=0, tiled=True)
    symmetric = (error_full + error_full.T).astype(jnp.bfloat16)
    upstream = jnp.dot(features, symmetric, preferred_element_type=jnp.float32) / math.sqrt(
        out_width
    )
    grad_pre = (
        (upstream * gelu_grad(preact)).astype(jnp.bfloat16).reshape(tile_rows, tile_cols, out_width)
    )
    grad_padded = padded_2(grad_pre, (("rows", 0), ("cols", 1)), 1)
    flipped = conv_weight[::-1, ::-1].transpose(0, 1, 3, 2).reshape(9 * out_width, in_width)
    grad_canvas = jnp.dot(
        patches(grad_padded, tile_rows, tile_cols), flipped, preferred_element_type=jnp.float32
    )
    return (gram_own, grad_canvas.astype(jnp.bfloat16).reshape(tile_rows, tile_cols, in_width))


def solution(mesh):
    return jax.shard_map(
        on_device,
        mesh=mesh,
        in_specs=(P("rows", "cols", None), P(), P(), P(("rows", "cols"), None)),
        out_specs=(P(("rows", "cols"), None), P("rows", "cols", None)),
        check_vma=False,
    )
```

profile of v0, /device:TPU:33, one launch (start us, length us, event | category | flops | bytes accessed | tf_op | source)
XLA Modules:
  0.0 724.9 jit_solution(6664298643092920723)
XLA Ops:
  7.2 0.9 fusion.43
  8.2 3.1 collective-permute-start
  11.3 6.4 collective-permute-start.1
  17.7 1.1 constant_dynamic-update-slice_fusion.1
  19.0 6.6 collective-permute-start.2
  25.6 0.7 convert_element_type.15
  26.3 1.9 collective-permute-start.3
  28.4 3.8 collective-permute-done.3
  33.0 1.2 copy-done.1
  34.2 2.6 fusion.44
  36.8 1.3 copy-done.4
  38.1 2.8 fusion.30
  40.9 255.6 %all-reduce.3.cloned.1.call-done = f32[512,512]{1,0:T(8,128)} async-done(((f32[512,512]{1,0:T(8,128)}), f32[512,512]{1,0:T(8,128)}) %all-reduce.3.cloned.1.call-update) | async-done | bytes 1048592
  296.5 1.3 subtract_bitcast_fusion
  297.8 379.7 %all-gather.3.cloned.1.call-done = f32[256,2,512]{2,1,0:T(2,128)} async-done(((f32[1,2,512]{2,1,0:T(2,128)}), f32[256,2,512]{2,1,0:T(2,128)}) %all-gather.3.cloned.1.call-update) | async-done | bytes 1048592 | tf_op jit(solution)/shard_map/all_gather | solution.py:61
  677.5 1.9 reshape.39
  679.5 0.3 copy.9
  679.8 4.5 fusion.14
  684.3 0.7 slice_bitcast_fusion.1
  685.0 5.2 collective-permute-start.5
  690.3 1.9 collective-permute-start.4
  692.2 2.8 copy.10
  695.0 1.6 rev.3
  696.6 4.5 collective-permute-done.4
  701.2 0.7 pad_maximum_fusion.7
  701.9 3.3 collective-permute-start.7
  705.3 3.6 collective-permute-start.6
  708.9 1.1 pad_maximum_fusion.1
  710.0 1.6 pad_maximum_fusion
  711.6 0.8 fusion.40
  713.1 1.5 copy-done.2
  714.6 3.4 convolution_convert_fusion
  (38 shorter events, 1.9 us)
Async XLA Ops:
  7.2 21.2 %copy-start = (bf16[8,128,256]{2,1,0:T(8,128)(2,1)S(1)}, bf16[8,128,256]{2,1,0:T(8,128)(2,1)}, u32[]{:S(2)}) copy-start(bf16[8,128,256]{2,1,0:T(8,128)(2,1)} %param.4) | copy-start | bytes 1572868
  7.2 289.3 %all-reduce.3.cloned.1.call-start = ((), (), s32[]{:S(2)}) async-start(), calls=%async_computation.1 | async-start | bytes 2097152
  8.2 9.5 %collective-permute-start = (bf16[1,128,256]{2,1,0:T(8,128)(2,1)S(1)}, bf16[1,128,256]{2,1,0:T(8,128)(2,1)S(1)}, u32[]{:S(2)}, u32[]{:S(2)}) collective-permute-start(bf16[1,128,256]{2,1,0:T(8,128)(2,1)S(1)} %get-tuple-element.21), channel_id=1, source_target_pairs={{0,8},{8,16},{16,24},{24,32},{32,40},{40,48},{48,56},{56,64},{64,7... | collective-permute-start | bytes 196616 | tf_op jit(solution)/shard_map/ppermute | solution.py:15
  11.3 7.7 %collective-permute-start.1 = (bf16[1,128,256]{2,1,0:T(8,128)(2,1)S(1)}, bf16[1,128,256]{2,1,0:T(8,128)(2,1)S(1)}, u32[]{:S(2)}, u32[]{:S(2)}) collective-permute-start(bf16[1,128,256]{2,1,0:T(8,128)(2,1)S(1)} %get-tuple-element.20), channel_id=1, source_target_pairs={{8,0},{16,8},{24,16},{32,24},{40,32},{48,40},{56,48},{64,56},{72,6... | collective-permute-start | bytes 196616 | tf_op jit(solution)/shard_map/ppermute | solution.py:18
  19.0 9.2 %collective-permute-start.2 = (bf16[10,1,256]{2,1,0:T(2,128)(2,1)S(1)}, bf16[10,1,256]{2,1,0:T(2,128)(2,1)S(1)}, u32[]{:S(2)}, u32[]{:S(2)}) collective-permute-start(bf16[10,1,256]{2,1,0:T(2,128)(2,1)S(1)} %get-tuple-element.19), channel_id=1, source_target_pairs={{0,1},{1,2},{2,3},{3,4},{4,5},{5,6},{6,7},{8,9},{9,10},{10,11},{11... | collective-permute-start | bytes 15368 | tf_op jit(solution)/shard_map/ppermute | solution.py:15
  26.3 5.9 collective-permute-start.3
  32.5 1.7 copy-start.1
  36.8 1.3 copy-start.4
  38.1 258.4 %copy-start.3 = (f32[2,512]{1,0:T(2,128)S(1)}, f32[2,512]{1,0:T(2,128)}, u32[]{:S(2)}) copy-start(f32[2,512]{1,0:T(2,128)} %param.7) | copy-start | bytes 12292
  40.9 636.6 %all-gather.3.cloned.1.call-start = ((), (), s32[]{:S(2)}) async-start(), calls=%async_computation | async-start | bytes 1052672 | tf_op jit(solution)/shard_map/all_gather | solution.py:61
  685.0 11.6 %collective-permute-start.5 = (bf16[1,128,512]{2,1,0:T(8,128)(2,1)}, bf16[1,128,512]{2,1,0:T(8,128)(2,1)S(1)}, u32[]{:S(2)}, u32[]{:S(2)}) collective-permute-start(bf16[1,128,512]{2,1,0:T(8,128)(2,1)} %get-tuple-element.17), channel_id=1, source_target_pairs={{8,0},{16,8},{24,16},{32,24},{40,32},{48,40},{56,48},{64,56},{72,6... | collective-permute-start | bytes 393224 | tf_op jit(solution)/shard_map/ppermute | solution.py:18
  690.3 10.9 %collective-permute-start.4 = (bf16[1,128,512]{2,1,0:T(8,128)(2,1)}, bf16[1,128,512]{2,1,0:T(8,128)(2,1)}, u32[]{:S(2)}, u32[]{:S(2)}) collective-permute-start(bf16[1,128,512]{2,1,0:T(8,128)(2,1)} %get-tuple-element.16), channel_id=1, source_target_pairs={{0,8},{8,16},{16,24},{24,32},{32,40},{40,48},{48,56},{56,64},{64,7... | collective-permute-start | bytes 393224 | tf_op jit(solution)/shard_map/ppermute | solution.py:15
  701.9 8.1 %collective-permute-start.7 = (bf16[10,1,512]{2,1,0:T(2,128)(2,1)S(1)}, bf16[10,1,512]{2,1,0:T(2,128)(2,1)S(1)}, u32[]{:S(2)}, u32[]{:S(2)}) collective-permute-start(bf16[10,1,512]{2,1,0:T(2,128)(2,1)S(1)} %get-tuple-element.12), channel_id=1, source_target_pairs={{1,0},{2,1},{3,2},{4,3},{5,4},{6,5},{7,6},{9,8},{10,9},{11,10},{12... | collective-permute-start | bytes 30728 | tf_op jit(solution)/shard_map/ppermute | solution.py:18
  705.3 4.8 collective-permute-start.6
  713.0 1.7 copy-start.2
Sparse Core Ops, SparseCore 0:
  41.0 255.4 all-reduce.2
  299.0 378.4 all-gather.2
where the time goes:
time: 726 us; the launch traced here: 725 us
  waiting for transfers between devices  644 us (89%)
  starting transfers between devices  32.2 us (4%)
  local copies, waits for them, and re-layouts  15 us (2%)
  between operations  14.4 us (2%)
  matrix products  13.3 us (2%)
    all_gather x1, waiting for transfers between devices, on_device(): error_full = lax.all_gather(error_own, ('rows', 'cols'), axis=0, tiled=True)  380 us
    unnamed x3, waiting for transfers between devices  256 us
    ppermute x4, starting transfers between devices, padded_2(): lax.ppermute(lax.slice_in_dim(block, 0, width, axis=dim), axis, backward)  16.8 us
    ppermute x4, starting transfers between devices, padded_2(): lax.ppermute(lax.slice_in_dim(block, block.shape[dim] - width, None, axis...  15.3 us
  transfers between devices with their start and end apart: 10, of which 5 were waited for; matrix products, arithmetic and copies ran while one was open for 1% of the time, Pallas kernels for 0%

commit v1 on v0

--- a/solution.py
+++ b/solution.py
@@ -58,7 +58,10 @@
         / pixel_total
     )
     error_own = gram_own - target_gram
-    error_full = lax.all_gather(error_own, ("rows", "cols"), axis=0, tiled=True)
+    size = lax.axis_size(("rows", "cols"))
+    parts = jnp.stack([error_own for _ in range(size)])
+    parts = lax.all_to_all(parts, ("rows", "cols"), split_axis=0, concat_axis=0)
+    error_full = jnp.concatenate(parts, axis=0)
     symmetric = (error_full + error_full.T).astype(jnp.bfloat16)
     upstream = jnp.dot(features, symmetric, preferred_element_type=jnp.float32) / math.sqrt(
         out_width

time: 726 us -> 386 us (0.53)
  waiting for transfers between devices: 644 us -> 263 us
  blocking collectives: 0 us -> 43.3 us
    all_gather x1 -> x0, waiting for transfers between devices: 380 us -> none  [on_device(): error_full = lax.all_gather(error_own, ('rows', 'cols'), axis=0, tiled=True)]
    all_to_all x0 -> x1, blocking collectives: none -> 43.3 us  [on_device(): parts = lax.all_to_all(parts, ('rows', 'cols'), split_axis=0, concat_axis=0)]
    unnamed x3 -> x2, waiting for transfers between devices: 256 us -> 256 us
  transfers between devices with their start and end apart: 10 -> 9, of which waited for: 5 -> 4; matrix products, arithmetic and copies ran while one was open for 1% -> 2% of each run, Pallas kernels for 0% -> 0%
where the time goes in v1:
time: 386 us
  waiting for transfers between devices  263 us (68%)
  blocking collectives  43.3 us (11%)
  starting transfers between devices  31 us (8%)
  between operations  14.4 us (4%)
  local copies, waits for them, and re-layouts  14 us (4%)
  matrix products  13.3 us (3%)
  other arithmetic  6.28 us (2%)
    unnamed x2, waiting for transfers between devices  256 us
    all_to_all x1, blocking collectives, on_device(): parts = lax.all_to_all(parts, ('rows', 'cols'), split_axis=0, concat_axis=0)  43.3 us
    ppermute x4, starting transfers between devices, padded_2(): lax.ppermute(lax.slice_in_dim(block, 0, width, axis=dim), axis, backward)  16.6 us
    ppermute x4, starting transfers between devices, padded_2(): lax.ppermute(lax.slice_in_dim(block, block.shape[dim] - width, None, axis...  14.3 us
    unnamed x22, local copies, waits for them, and re-layouts  8.54 us
  transfers between devices with their start and end apart: 9, of which 4 were waited for; matrix products, arithmetic and copies ran while one was open for 2% of the time, Pallas kernels for 0%

profile of v1, /device:TPU:33, one launch (start us, length us, event | category | flops | bytes accessed | tf_op | source)
XLA Modules:
  0.0 385.6 jit_solution(4199634923770314276)
XLA Ops:
  7.2 0.9 fusion.44
  8.2 3.1 collective-permute-start
  11.3 6.4 %collective-permute-start.1 = (bf16[1,128,256]{2,1,0:T(8,128)(2,1)S(1)}, bf16[1,128,256]{2,1,0:T(8,128)(2,1)S(1)}, u32[]{:S(2)}, u32[]{:S(2)}) collective-permute-start(bf16[1,128,256]{2,1,0:T(8,128)(2,1)S(1)} %get-tuple-element.20), channel_id=1, source_target_pairs={{8,0},{16,8},{24,16},{32,24},{40,32},{48,40},{56,48},{64,56},{72,6... | collective-permute-start | bytes 196616 | tf_op jit(solution)/shard_map/ppermute | solution.py:18
  17.7 1.1 constant_dynamic-update-slice_fusion.1
  19.0 6.6 %collective-permute-start.2 = (bf16[10,1,256]{2,1,0:T(2,128)(2,1)S(1)}, bf16[10,1,256]{2,1,0:T(2,128)(2,1)S(1)}, u32[]{:S(2)}, u32[]{:S(2)}) collective-permute-start(bf16[10,1,256]{2,1,0:T(2,128)(2,1)S(1)} %get-tuple-element.19), channel_id=1, source_target_pairs={{0,1},{1,2},{2,3},{3,4},{4,5},{5,6},{6,7},{8,9},{9,10},{10,11},{11... | collective-permute-start | bytes 15368 | tf_op jit(solution)/shard_map/ppermute | solution.py:15
  25.6 0.7 convert_element_type.15
  26.3 1.9 collective-permute-start.3
  28.4 3.8 collective-permute-done.3
  33.0 1.2 copy-done.1
  34.2 2.6 fusion.45
  36.8 1.3 copy-done.4
  38.1 2.8 fusion.30
  40.9 255.6 %all-reduce.3.cloned.1.call-done = f32[512,512]{1,0:T(8,128)} async-done(((f32[512,512]{1,0:T(8,128)}), f32[512,512]{1,0:T(8,128)}) %all-reduce.3.cloned.1.call-update) | async-done | bytes 1048592
  296.5 1.3 fusion.40
  298.1 43.3 %all_to_all.5 = f32[256,2,512]{2,1,0:T(2,128)S(1)} all-to-all(f32[256,2,512]{2,1,0:T(2,128)S(1)} %stack.2), channel_id=1, replica_groups=mesh['rows'=32,'cols'=8] {'rows','cols'}, dimensions={0} | all-to-all | bytes 2097152 | tf_op jit(solution)/shard_map/all_to_all | solution.py:63
  341.5 0.7 reshape.40
  342.2 0.3 copy.9
  342.5 4.5 %fusion.14 = bf16[1024,512]{1,0:T(8,128)(2,1)S(1)} fusion(f32[1024,512]{1,0:T(8,128)} %copy-done.4, f32[512]{0:T(512)S(1)} %convert_element_type.15, f32[512,512]{1,0:T(8,128)S(1)} %reshape.40, f32[512,512]{0,1:T(8,128)S(1)} %copy.9), kind=kOutput, calls=%fused_computation.17 | convolution fusion | flops 553648128 | bytes 5244928 | tf_op jit(solution)/shard_map/dot_general | solution.py:66
  347.0 0.7 slice_bitcast_fusion.1
  347.7 3.2 collective-permute-start.5
  351.0 2.1 collective-permute-start.4
  353.0 2.8 copy.10
  355.9 1.6 rev.3
  357.5 3.7 collective-permute-done.4
  361.2 0.7 pad_maximum_fusion.7
  362.0 5.1 %collective-permute-start.7 = (bf16[10,1,512]{2,1,0:T(2,128)(2,1)S(1)}, bf16[10,1,512]{2,1,0:T(2,128)(2,1)S(1)}, u32[]{:S(2)}, u32[]{:S(2)}) collective-permute-start(bf16[10,1,512]{2,1,0:T(2,128)(2,1)S(1)} %get-tuple-element.12), channel_id=1, source_target_pairs={{1,0},{2,1},{3,2},{4,3},{5,4},{6,5},{7,6},{9,8},{10,9},{11,10},{12... | collective-permute-start | bytes 30728 | tf_op jit(solution)/shard_map/ppermute | solution.py:18
  367.1 2.6 collective-permute-start.6
  369.6 1.1 pad_maximum_fusion.1
  370.8 1.6 pad_maximum_fusion
  372.3 0.8 fusion.41
  373.9 1.5 copy-done.2
  375.4 3.4 convolution_convert_fusion
  (37 shorter events, 2.1 us)
Async XLA Ops:
  7.2 21.2 %copy-start = (bf16[8,128,256]{2,1,0:T(8,128)(2,1)S(1)}, bf16[8,128,256]{2,1,0:T(8,128)(2,1)}, u32[]{:S(2)}) copy-start(bf16[8,128,256]{2,1,0:T(8,128)(2,1)} %param.4) | copy-start | bytes 1572868
  7.2 289.4 %all-reduce.3.cloned.1.call-start = ((), (), s32[]{:S(2)}) async-start(), calls=%async_computation.1 | async-start | bytes 2097152
  8.2 9.5 %collective-permute-start = (bf16[1,128,256]{2,1,0:T(8,128)(2,1)S(1)}, bf16[1,128,256]{2,1,0:T(8,128)(2,1)S(1)}, u32[]{:S(2)}, u32[]{:S(2)}) collective-permute-start(bf16[1,128,256]{2,1,0:T(8,128)(2,1)S(1)} %get-tuple-element.21), channel_id=1, source_target_pairs={{0,8},{8,16},{16,24},{24,32},{32,40},{40,48},{48,56},{56,64},{64,7... | collective-permute-start | bytes 196616 | tf_op jit(solution)/shard_map/ppermute | solution.py:15
  11.3 7.7 %collective-permute-start.1 = (bf16[1,128,256]{2,1,0:T(8,128)(2,1)S(1)}, bf16[1,128,256]{2,1,0:T(8,128)(2,1)S(1)}, u32[]{:S(2)}, u32[]{:S(2)}) collective-permute-start(bf16[1,128,256]{2,1,0:T(8,128)(2,1)S(1)} %get-tuple-element.20), channel_id=1, source_target_pairs={{8,0},{16,8},{24,16},{32,24},{40,32},{48,40},{56,48},{64,56},{72,6... | collective-permute-start | bytes 196616 | tf_op jit(solution)/shard_map/ppermute | solution.py:18
  19.0 9.2 %collective-permute-start.2 = (bf16[10,1,256]{2,1,0:T(2,128)(2,1)S(1)}, bf16[10,1,256]{2,1,0:T(2,128)(2,1)S(1)}, u32[]{:S(2)}, u32[]{:S(2)}) collective-permute-start(bf16[10,1,256]{2,1,0:T(2,128)(2,1)S(1)} %get-tuple-element.19), channel_id=1, source_target_pairs={{0,1},{1,2},{2,3},{3,4},{4,5},{5,6},{6,7},{8,9},{9,10},{10,11},{11... | collective-permute-start | bytes 15368 | tf_op jit(solution)/shard_map/ppermute | solution.py:15
  26.3 5.9 %collective-permute-start.3 = (bf16[10,1,256]{2,1,0:T(2,128)(2,1)S(1)}, bf16[10,1,256]{2,1,0:T(2,128)(2,1)S(1)}, u32[]{:S(2)}, u32[]{:S(2)}) collective-permute-start(bf16[10,1,256]{2,1,0:T(2,128)(2,1)S(1)} %get-tuple-element.18), channel_id=1, source_target_pairs={{1,0},{2,1},{3,2},{4,3},{5,4},{6,5},{7,6},{9,8},{10,9},{11,10},{12... | collective-permute-start | bytes 15368 | tf_op jit(solution)/shard_map/ppermute | solution.py:18
  32.5 1.7 copy-start.1
  36.8 1.3 copy-start.4
  38.1 258.4 %copy-start.3 = (f32[2,512]{1,0:T(2,128)S(1)}, f32[2,512]{1,0:T(2,128)}, u32[]{:S(2)}) copy-start(f32[2,512]{1,0:T(2,128)} %param.7) | copy-start | bytes 12292
  347.7 9.7 %collective-permute-start.5 = (bf16[1,128,512]{2,1,0:T(8,128)(2,1)}, bf16[1,128,512]{2,1,0:T(8,128)(2,1)S(1)}, u32[]{:S(2)}, u32[]{:S(2)}) collective-permute-start(bf16[1,128,512]{2,1,0:T(8,128)(2,1)} %get-tuple-element.17), channel_id=1, source_target_pairs={{8,0},{16,8},{24,16},{32,24},{40,32},{48,40},{56,48},{64,56},{72,6... | collective-permute-start | bytes 393224 | tf_op jit(solution)/shard_map/ppermute | solution.py:18
  351.0 10.2 %collective-permute-start.4 = (bf16[1,128,512]{2,1,0:T(8,128)(2,1)}, bf16[1,128,512]{2,1,0:T(8,128)(2,1)}, u32[]{:S(2)}, u32[]{:S(2)}) collective-permute-start(bf16[1,128,512]{2,1,0:T(8,128)(2,1)} %get-tuple-element.16), channel_id=1, source_target_pairs={{0,8},{8,16},{16,24},{24,32},{32,40},{40,48},{48,56},{56,64},{64,7... | collective-permute-start | bytes 393224 | tf_op jit(solution)/shard_map/ppermute | solution.py:15
  362.0 8.8 %collective-permute-start.7 = (bf16[10,1,512]{2,1,0:T(2,128)(2,1)S(1)}, bf16[10,1,512]{2,1,0:T(2,128)(2,1)S(1)}, u32[]{:S(2)}, u32[]{:S(2)}) collective-permute-start(bf16[10,1,512]{2,1,0:T(2,128)(2,1)S(1)} %get-tuple-element.12), channel_id=1, source_target_pairs={{1,0},{2,1},{3,2},{4,3},{5,4},{6,5},{7,6},{9,8},{10,9},{11,10},{12... | collective-permute-start | bytes 30728 | tf_op jit(solution)/shard_map/ppermute | solution.py:18
  367.1 3.7 collective-permute-start.6
  373.7 1.7 copy-start.2
Sparse Core Ops, SparseCore 0:
  41.0 255.4 all-reduce.2
